TPU v7x, 32 devices: a whole 2x2x4 slice. The times are simulated.
32 devices in a mesh: groups: 2 (over y), passage: 8 (over z, x), tensor: 2 (over core).
Axes of the slice: x: 2, y: 2, z: 4, core: 2. Of those that a mesh axis runs over, the one named last changes fastest.
Arguments:
- corpus: bfloat16 [96, 256, 1024], P(('groups', 'passage')), parts along dimension 0, may hold values from -6 to 6
- queries: bfloat16 [32, 2048], P(('groups', 'passage'), 'tensor'), parts along dimension 0, may hold values from -180 to 180
- key_weight: bfloat16 [1024, 2048], P('passage', 'tensor'), may hold values from -0.1875 to 0.1875
- value_weight: bfloat16 [1024, 2048], P('passage', 'tensor'), may hold values from -0.1875 to 0.1875
- retrieved: int32 [2, 16], P('groups'), parts along dimension 0, may hold values from 0 to 47, as said below
- placement_map: int32 [96], P('groups'), parts along dimension 0, may hold values from 0 to 47, as said below
- valid_counts: int32 [96], P('groups'), parts along dimension 0, may hold values from 16 to 256
Outputs:
- context: bfloat16 [32, 2048], P(('groups', 'passage'), 'tensor'), parts along dimension 0
There are 2 independent parts, one for each index of `groups`. A program takes and returns all parts, laid end to end along the dimension named above; an argument that names none is the same for every part. Nothing has to cross between parts.
Inputs may be any that keep to these rules, and one draw needn't show every extreme that they name: Each row lists 16 ids; all 16 retrieved ids are distinct. With shard = placement_map[id] // 6, at most 5 retrieved passages lie on one shard, and some shard holds exactly 5. `placement_map`: A permutation of the corpus rows.
All inputs are finite; a program needn't handle non-finite values.
Results may differ from a plain program's by a relative error of at most 0.01.
The roundings to bfloat16 on the way count: a program that leaves them out, or rounds other values in their place, can miss the bound.
Values may be sent and summed in bfloat16 or wider, within the bound.
A program may use at most 64 MiB of HBM per device.

v0:
```python
import jax
import jax.numpy as jnp
from jax import lax
from jax.sharding import PartitionSpec as P

DH = 64
LEN = 256
MOST = 5
QT = 16


def normalize(hidden):
    values32 = hidden.astype(jnp.float32)
    factor = lax.rsqrt(jnp.mean(values32 * values32, axis=-1, keepdims=True) + 1e-06)
    return (values32 * factor).astype(jnp.bfloat16)


def widen(stats):
    return jnp.repeat(stats, DH, axis=-1)


def join_partials(first, second):
    top_one, mass_one, ctx_one = first
    top_two, mass_two, ctx_two = second
    highest = jnp.maximum(top_one, top_two)
    scale_one = jnp.exp(top_one - highest)
    scale_two = jnp.exp(top_two - highest)
    return (
        highest,
        mass_one * scale_one + mass_two * scale_two,
        ctx_one * widen(scale_one) + ctx_two * widen(scale_two),
    )


def on_device(corpus, queries, key_weight, value_weight, retrieved, placement_map, valid_counts):
    shard_index = lax.axis_index("passage")
    corp_rows = corpus.shape[0]
    per_question = retrieved.shape[1]
    total_ret = retrieved.shape[0] * per_question
    flat_ids = retrieved.reshape(total_ret)
    corpus_row = placement_map[flat_ids]
    lengths = valid_counts[flat_ids]
    owned_mask = corpus_row // corp_rows == shard_index
    owner_rank = jnp.cumsum(owned_mask.astype(jnp.int32)) - 1
    slot_iota = jnp.arange(MOST, dtype=jnp.int32)
    selector = (owned_mask[None, :] & (owner_rank[None, :] == slot_iota[:, None])).astype(jnp.int32)
    local_rows = jnp.sum(selector * (corpus_row % corp_rows)[None, :], axis=1)
    slot_lengths = jnp.sum(selector * lengths[None, :], axis=1)
    question_ids = jnp.arange(total_ret, dtype=jnp.int32) // per_question
    slot_question = jnp.sum(selector * question_ids[None, :], axis=1)
    passages = corpus[local_rows]
    normed = normalize(passages).reshape(MOST * LEN, passages.shape[2])
    full_key, full_value = (
        lax.all_gather(key_weight, "passage", axis=0, tiled=True),
        lax.all_gather(value_weight, "passage", axis=0, tiled=True),
    )
    width = key_weight.shape[1]
    heads = width // DH
    key_rows = jnp.dot(normed, full_key, preferred_element_type=jnp.float32).astype(jnp.bfloat16)
    value_rows = jnp.dot(normed, full_value, preferred_element_type=jnp.float32).astype(
        jnp.bfloat16
    )
    key_rows = key_rows.reshape(MOST, LEN, heads, DH)
    value_rows = value_rows.reshape(MOST, LEN, heads, DH)
    all_queries = lax.all_gather(queries, "passage", axis=0, tiled=True)
    query_total = all_queries.shape[0]
    best_score = jnp.full((query_total, heads), -1e30, jnp.float32)
    row_total = jnp.zeros((query_total, heads), jnp.float32)
    context_sum = jnp.zeros((query_total, width), jnp.float32)
    positions = jnp.arange(LEN, dtype=jnp.int32)
    scaling = DH ** (-0.5)
    for number in range(MOST):
        first_row = slot_question[number] * QT
        block = lax.dynamic_slice_in_dim(all_queries, first_row, QT, 0).reshape(QT, heads, DH)
        scores = (
            jnp.einsum("thd,lhd->htl", block, key_rows[number], preferred_element_type=jnp.float32)
            * scaling
        )
        live_mask = (positions < slot_lengths[number])[None, None, :]
        scores = jnp.where(live_mask, scores, jnp.float32(-1e30))
        top_score = jnp.max(scores, axis=-1)
        weights = jnp.where(live_mask, jnp.exp(scores - top_score[..., None]), jnp.float32(0.0))
        row_mass = jnp.sum(weights, axis=-1)
        partial_ctx = jnp.einsum(
            "htl,lhd->thd",
            weights.astype(jnp.bfloat16),
            value_rows[number],
            preferred_element_type=jnp.float32,
        ).reshape(QT, width)
        old_state = (
            lax.dynamic_slice_in_dim(best_score, first_row, QT, 0),
            lax.dynamic_slice_in_dim(row_total, first_row, QT, 0),
            lax.dynamic_slice_in_dim(context_sum, first_row, QT, 0),
        )
        new_top, new_mass, new_ctx = join_partials(
            old_state, (top_score.T, row_mass.T, partial_ctx)
        )
        best_score = lax.dynamic_update_slice_in_dim(best_score, new_top, first_row, 0)
        row_total = lax.dynamic_update_slice_in_dim(row_total, new_mass, first_row, 0)
        context_sum = lax.dynamic_update_slice_in_dim(context_sum, new_ctx, first_row, 0)
    global_top = lax.pmax(best_score, "passage")
    rescale = jnp.exp(best_score - global_top)
    own_mass, own_ctx = (
        lax.psum_scatter(row_total * rescale, "passage", scatter_dimension=0, tiled=True),
        lax.psum_scatter(context_sum * widen(rescale), "passage", scatter_dimension=0, tiled=True),
    )
    return (own_ctx / widen(own_mass)).astype(jnp.bfloat16)


def solution(mesh):
    in_specs = (
        P(("groups", "passage"), None, None),
        P(("groups", "passage"), "tensor"),
        P("passage", "tensor"),
        P("passage", "tensor"),
        P("groups", None),
        P("groups"),
        P("groups"),
    )
    out_specs = P(("groups", "passage"), "tensor")
    return jax.shard_map(
        on_device, mesh=mesh, in_specs=in_specs, out_specs=out_specs, check_vma=False
    )
```

profile of v0, /device:TPU:0, one launch (start us, length us, event | category | flops | bytes accessed | tf_op | source)
XLA Modules:
  0.0 196.4 jit_solution(11612404778578878747)
XLA Ops:
  6.5 0.7 all-gather.4.cloned.1.call-update
  7.3 0.7 all-gather.6.cloned.1.call-update
  8.1 0.7 fusion.84
  8.7 1.3 gather_fusion
  10.4 1.3 gather_fusion.1
  11.9 2.4 %gather_fusion.2 = bf16[5,256,1024]{2,1,0:T(8,128)(2,1)} fusion(bf16[6,256,1024]{2,1,0:T(8,128)(2,1)S(1)} %copy-done, s32[1024]{0:T(1024)S(1)} %pad_clamp_fusion), kind=kCustom, calls=%fused_computation.2 | custom fusion | bytes 5242900 | tf_op jit(solution)/shard_map/gather | solution.py:51
  14.3 2.3 %multiply_reduce_fusion = f32[5,256]{1,0:T(8,128)S(1)} fusion(bf16[5,256,1024]{2,1,0:T(8,128)(2,1)} %gather_fusion.2), kind=kLoop, calls=%fused_computation.5 | loop fusion | flops 3930880 | bytes 2626560 | tf_op jit(solution)/shard_map/reduce_sum | solution.py:14
  16.7 0.7 fusion.99
  17.3 0.7 iota_compare_fusion.4
  18.0 32.4 %all-gather = bf16[8,2,1024]{2,1,0:T(2,128)(2,1)S(1)} all-gather(bf16[1,2,1024]{2,1,0:T(2,128)(2,1)S(1)} %bitcast.194), channel_id=1, replica_groups=mesh['groups'=2,'passage'=8,'tensor'=2] {'passage'}, dimensions={0}, use_global_device_ids=true | all-gather | bytes 36864 | tf_op jit(solution)/shard_map/all_gather | solution.py:65
  50.6 0.6 dynamic-slice
  51.9 0.7 iota_compare_fusion.5
  52.5 0.6 iota_compare_fusion.2
  53.2 0.6 iota_compare_fusion.3
  53.8 0.6 iota_compare_fusion.1
  54.4 3.8 %fusion = bf16[1280,1024]{1,0:T(8,128)(2,1)} fusion(f32[1280]{0:T(1024)S(1)} %rsqrt.12, bf16[5,256,1024]{2,1,0:T(8,128)(2,1)} %gather_fusion.2), kind=kLoop, calls=%fused_computation.4 | loop fusion | flops 3932160 | bytes 5248000 | tf_op jit(solution)/shard_map/convert_element_type | solution.py:15
  58.2 3.6 %all-gather.4.cloned.1.call-done = bf16[1024,1024]{1,0:T(8,128)(2,1)} async-done(((bf16[128,1024]{1,0:T(8,128)(2,1)}), bf16[1024,1024]{1,0:T(8,128)(2,1)}) %all-gather.4.cloned.1.call-update) | async-done | bytes 2097168 | tf_op jit(solution)/shard_map/all_gather | solution.py:54
  61.8 5.3 %convolution_convert_fusion.1 = bf16[1280,1024]{0,1:T(8,128)(2,1)S(1)} fusion(bf16[1280,1024]{1,0:T(8,128)(2,1)} %fusion, bf16[1024,1024]{1,0:T(8,128)(2,1)} %all-gather.4.cloned.1.call-done), kind=kOutput, calls=%fused_computation.7 | convolution fusion | flops 2685665280 | bytes 7340032 | tf_op jit(solution)/shard_map/dot_general | solution.py:59
  67.3 0.9 fusion.104
  68.2 0.9 fusion.100
  69.4 0.9 fusion.103
  70.3 0.9 fusion.101
  71.2 19.5 %pmax.7 = f32[16,16]{0,1:T(8,128)S(1)} all-reduce(f32[16,16]{0,1:T(8,128)S(1)} %get-tuple-element.17), channel_id=1, replica_groups=mesh['groups'=2,'passage'=8,'tensor'=2] {'passage'}, use_global_device_ids=true, to_apply=%region_9.10 | all-reduce | flops 256 | bytes 2048 | tf_op jit(solution)/shard_map/pmax | solution.py:101
  90.7 1.1 fusion.34
  91.8 20.2 %all-gather.6.cloned.1.call-done = bf16[1024,1024]{1,0:T(8,128)(2,1)} async-done(((bf16[128,1024]{1,0:T(8,128)(2,1)}), bf16[1024,1024]{1,0:T(8,128)(2,1)}) %all-gather.6.cloned.1.call-update) | async-done | bytes 2097168 | tf_op jit(solution)/shard_map/all_gather | solution.py:55
  112.0 5.3 %convolution_convert_fusion = bf16[1280,1024]{0,1:T(8,128)(2,1)S(1)} fusion(bf16[1280,1024]{1,0:T(8,128)(2,1)} %fusion, bf16[1024,1024]{1,0:T(8,128)(2,1)} %all-gather.6.cloned.1.call-done), kind=kOutput, calls=%fused_computation.6 | convolution fusion | flops 2685665280 | bytes 7340032 | tf_op jit(solution)/shard_map/dot_general | solution.py:60
  117.6 0.7 copy-done.2
  119.9 0.3 fusion.16
  120.7 0.7 reshape.298
  121.4 19.2 %all-reduce.1 = f32[16,16]{0,1:T(8,128)S(1)} all-reduce(f32[16,16]{0,1:T(8,128)S(1)} %get-tuple-element.34), channel_id=3, replica_groups=mesh['groups'=2,'passage'=8,'tensor'=2] {'passage'}, use_global_device_ids=true, to_apply=%region_16.17.clone | all-reduce | flops 256 | bytes 2048
  141.0 47.6 %all-reduce.4.cloned.1.call-done = f32[16,1024]{1,0:T(8,128)} async-done(((f32[16,1024]{1,0:T(8,128)}), f32[16,1024]{1,0:T(8,128)}) %all-reduce.4.cloned.1.call-update) | async-done | bytes 65552
  188.6 1.4 fusion.81
  (51 shorter events, 3.7 us)
Async XLA Ops:
  6.5 5.4 %copy-start = (bf16[6,256,1024]{2,1,0:T(8,128)(2,1)S(1)}, bf16[6,256,1024]{2,1,0:T(8,128)(2,1)}, u32[]{:S(2)}) copy-start(bf16[6,256,1024]{2,1,0:T(8,128)(2,1)} %param.7) | copy-start | bytes 9437188
  6.5 55.3 %all-gather.4.cloned.1.call-start = ((), (), s32[]{:S(2)}) async-start(), calls=%async_computation | async-start | bytes 2359296 | tf_op jit(solution)/shard_map/all_gather | solution.py:54
  7.3 104.8 %all-gather.6.cloned.1.call-start = ((), (), s32[]{:S(2)}) async-start(), calls=%async_computation.1 | async-start | bytes 2359296 | tf_op jit(solution)/shard_map/all_gather | solution.py:55
  8.0 180.6 %all-reduce.4.cloned.1.call-start = ((), (), s32[]{:S(2)}) async-start(), calls=%async_computation.2 | async-start | bytes 131072
  14.3 3.7 %copy-start.7 = (bf16[2,1024]{1,0:T(2,128)(2,1)S(1)}, bf16[2,1024]{1,0:T(2,128)(2,1)}, u32[]{:S(2)}) copy-start(bf16[2,1024]{1,0:T(2,128)(2,1)} %param.8) | copy-start | bytes 12292
  14.3 36.3 %copy-start.8 = (u32[32]{0:T(128)S(1)}, u32[32]{0:T(128)}, u32[]{:S(2)}) copy-start(u32[32]{0:T(128)} %constant.68) | copy-start | bytes 388
  54.4 36.3 %copy-start.5 = (pred[256]{0:T(512)(128)(4,1)}, pred[256]{0:T(512)(128)(4,1)S(1)}, u32[]{:S(2)}) copy-start(pred[256]{0:T(512)(128)(4,1)S(1)} %iota_compare_fusion.1) | copy-start | bytes 772
  117.4 1.0 copy-start.2
  117.4 1.0 copy-start.4
  117.4 1.3 copy-start.3
  118.7 1.6 copy-start.1
  118.7 1.6 copy-start.6
Sparse Core Ops, SparseCore 0:
  9.5 52.2 all-gather.3
  63.9 48.0 all-gather.5
  121.5 66.9 all-reduce.3
where the time goes:
time: 197 us; the launch traced here: 196 us
  waiting for transfers between devices  72.9 us (37%)
  blocking collectives  71.1 us (36%)
  matrix products  16.1 us (8%)
  between operations  14.1 us (7%)
  other arithmetic  13.3 us (7%)
  local copies, waits for them, and re-layouts  8.89 us (5%)
    unnamed x4, waiting for transfers between devices  49 us
    all_gather x1, blocking collectives, on_device(): all_queries = lax.all_gather(queries, 'passage', axis=0, tiled=True)  32.4 us
    all_gather x1, waiting for transfers between devices, on_device(): lax.all_gather(value_weight, 'passage', axis=0, tiled=True)  20.2 us
    pmax x1, blocking collectives, on_device(): global_top = lax.pmax(best_score, 'passage')  19.5 us
    unnamed x1, blocking collectives  19.2 us
    dot_general x1, matrix products, on_device(): jnp.dot(normed, full_key, preferred_element_type=jnp.float32)  5.32 us
    dot_general x1, matrix products, on_device(): jnp.dot(normed, full_value, preferred_element_type=jnp.float32)  5.31 us
  transfers between devices with their start and end apart: 3, of which 3 were waited for; matrix products, arithmetic and copies ran while one was open for 14% of the time, Pallas kernels for 0%

commit v1 on v0

--- a/solution.py
+++ b/solution.py
@@ -7,6 +7,23 @@
 LEN = 256
 MOST = 5
 QT = 16
+
+
+def _use_samples_all(z):
+    which_axis = "passage"
+    near = lax.axis_index(which_axis)
+    b_next = lax.axis_size(which_axis)
+    u_next, x_now = (b_next, near)
+    shaped, response = (z, 1)
+    while response < u_next:
+        mixed_arr = lax.ppermute(
+            shaped, axis_name=which_axis, perm=[(idx, idx ^ response) for idx in range(u_next)]
+        )
+        base_arr = jnp.concatenate([shaped, mixed_arr], axis=0)
+        f_next = jnp.concatenate([mixed_arr, shaped], axis=0)
+        shaped = jnp.where(x_now & response == 0, base_arr, f_next)
+        response = 2 * response
+    return shaped
 
 
 def normalize(hidden):
@@ -52,7 +69,7 @@
     normed = normalize(passages).reshape(MOST * LEN, passages.shape[2])
     full_key, full_value = (
         lax.all_gather(key_weight, "passage", axis=0, tiled=True),
-        lax.all_gather(value_weight, "passage", axis=0, tiled=True),
+        _use_samples_all(value_weight),
     )
     width = key_weight.shape[1]
     heads = width // DH

time: 197 us -> 254 us (1.29)
  blocking collectives: 71.1 us -> 119 us
  waiting for transfers between devices: 72.9 us -> 65.1 us
  starting transfers between devices: 0.08 us -> 7.39 us
  other arithmetic: 13.3 us -> 18 us
  matrix products: 16.1 us -> 19.2 us
    all_gather x1, blocking collectives: 32.4 us -> 82.5 us  [on_device(): all_queries = lax.all_gather(queries, 'passage', axis=0, tiled=True)]
    all_gather x1 -> x0, waiting for transfers between devices: 20.2 us -> none  [on_device(): lax.all_gather(value_weight, 'passage', axis=0, tiled=True)]
    ppermute x0 -> x3, waiting for transfers between devices: none -> 16.7 us  [_use_samples_all(): lax.ppermute(shaped, axis_name=which_axis, perm=[(idx, idx ^ response) fo...]
    ppermute x0 -> x3, starting transfers between devices: none -> 7.34 us  [_use_samples_all(): lax.ppermute(shaped, axis_name=which_axis, perm=[(idx, idx ^ response) fo...]
    select_n x0 -> x2, other arithmetic: none -> 5.01 us  [_use_samples_all(): shaped = jnp.where(x_now & response == 0, base_arr, f_next)]
    all_gather x1, waiting for transfers between devices: 3.64 us -> 0.01 us  [on_device(): lax.all_gather(key_weight, 'passage', axis=0, tiled=True)]
    dot_general x5, matrix products: 1.59 us -> 4.41 us  [on_device(): jnp.einsum('htl,lhd->thd', weights.astype(jnp.bfloat16), value_rows[numbe...]
    unnamed x4 -> x3, waiting for transfers between devices: 49 us -> 48.4 us
  transfers between devices with their start and end apart: 3 -> 5, of which waited for: 3 -> 3; matrix products, arithmetic and copies ran while one was open for 14% -> 11% of each run, Pallas kernels for 0% -> 0%
where the time goes in v1:
time: 254 us
  blocking collectives  119 us (47%)
  waiting for transfers between devices  65.1 us (26%)
  matrix products  19.2 us (8%)
  other arithmetic  18 us (7%)
  between operations  14.5 us (6%)
  local copies, waits for them, and re-layouts  10.1 us (4%)
  starting transfers between devices  7.39 us (3%)
    all_gather x1, blocking collectives, on_device(): all_queries = lax.all_gather(queries, 'passage', axis=0, tiled=True)  82.5 us
    unnamed x3, waiting for transfers between devices  48.4 us
    unnamed x1, blocking collectives  19.1 us
    pmax x1, blocking collectives, on_device(): global_top = lax.pmax(best_score, 'passage')  17.8 us
    ppermute x3, waiting for transfers between devices, _use_samples_all(): lax.ppermute(shaped, axis_name=which_axis, perm=[(idx, idx ^ response) fo...  16.7 us
    ppermute x3, starting transfers between devices, _use_samples_all(): lax.ppermute(shaped, axis_name=which_axis, perm=[(idx, idx ^ response) fo...  7.34 us
    dot_general x1, matrix products, on_device(): jnp.dot(normed, full_value, preferred_element_type=jnp.float32)  6.25 us
    dot_general x1, matrix products, on_device(): jnp.dot(normed, full_key, preferred_element_type=jnp.float32)  5.31 us
  transfers between devices with their start and end apart: 5, of which 3 were waited for; matrix products, arithmetic and copies ran while one was open for 11% of the time, Pallas kernels for 0%

profile of v1, /device:TPU:0, one launch (start us, length us, event | category | flops | bytes accessed | tf_op | source)
XLA Modules:
  0.0 253.7 jit_solution(4850664516846533297)
XLA Ops:
  6.5 0.7 all-gather.3.cloned.1.call-update
  7.3 3.0 %collective-permute-start = (bf16[128,1024]{1,0:T(8,128)(2,1)}, bf16[128,1024]{1,0:T(8,128)(2,1)S(1)}, u32[]{:S(2)}, u32[]{:S(2)}) collective-permute-start(bf16[128,1024]{1,0:T(8,128)(2,1)} %param.10), channel_id=1, source_target_pairs={{0,2},{2,0},{4,6},{6,4},{8,10},{10,8},{12,14},{14,12},{1,3},{3,1},... | collective-permute-start | bytes 786440 | tf_op jit(solution)/shard_map/ppermute | solution.py:19
  11.0 1.3 gather_fusion
  12.5 1.3 gather_fusion.1
  14.8 2.0 collective-permute-done
  16.8 2.0 maximum_select_fusion.3
  18.8 1.8 collective-permute-start.1
  21.3 2.4 gather_fusion.2
  23.6 2.4 multiply_reduce_fusion
  26.0 14.7 %collective-permute-done.1 = bf16[256,1024]{1,0:T(8,128)(2,1)} collective-permute-done((bf16[256,1024]{1,0:T(8,128)(2,1)}, bf16[256,1024]{1,0:T(8,128)(2,1)}, u32[]{:S(2)}, u32[]{:S(2)}) %collective-permute-start.1) | collective-permute-done | bytes 524320 | tf_op jit(solution)/shard_map/ppermute | solution.py:19
  40.7 3.0 %maximum_select_fusion.2 = bf16[512,1024]{1,0:T(8,128)(2,1)} fusion(bf16[256,1024]{1,0:T(8,128)(2,1)} %collective-permute-done.1, bf16[256,1024]{1,0:T(8,128)(2,1)} %maximum_select_fusion.3, pred[]{:T(512)S(6)} %eq.55), kind=kLoop, calls=%fused_computation.50 | loop fusion | flops 4718592 | bytes 2097153 | tf_op jit(solution)/shard_map/jit(_where)/select_n | solution.py:24
  43.7 2.5 collective-permute-start.2
  46.9 82.5 %all-gather = bf16[8,2,1024]{2,1,0:T(2,128)(2,1)S(1)} all-gather(bf16[1,2,1024]{2,1,0:T(2,128)(2,1)S(1)} %bitcast.193), channel_id=1, replica_groups=mesh['groups'=2,'passage'=8,'tensor'=2] {'passage'}, dimensions={0}, use_global_device_ids=true | all-gather | bytes 36864 | tf_op jit(solution)/shard_map/all_gather | solution.py:82
  131.4 0.7 iota_compare_fusion.3
  132.7 2.2 fusion
  135.0 6.2 %convolution_convert_fusion = bf16[1280,1024]{0,1:T(8,128)(2,1)S(1)} fusion(bf16[1280,1024]{1,0:T(8,128)(2,1)S(1)} %fusion, bf16[512,1024]{1,0:T(8,128)(2,1)} %collective-permute-done.2, bf16[512,1024]{1,0:T(8,128)(2,1)} %maximum_select_fusion.2, pred[]{:T(512)S(6)} %eq.54), kind=kOutput, calls=%fused_computation.6 | convolution fusion | flops 2695102464 | bytes 7340033 | tf_op jit(solution)/shard_map/dot_general | solution.py:77
  141.3 1.5 fusion.104
  142.8 5.3 %convolution_convert_fusion.1 = bf16[1280,1024]{0,1:T(8,128)(2,1)S(1)} fusion(bf16[1280,1024]{1,0:T(8,128)(2,1)} %copy-done.1, bf16[1024,1024]{1,0:T(8,128)(2,1)} %all-gather.3.cloned.1.call-done), kind=kOutput, calls=%fused_computation.7 | convolution fusion | flops 2685665280 | bytes 7340032 | tf_op jit(solution)/shard_map/dot_general | solution.py:76
  148.3 0.9 fusion.111
  149.2 0.9 fusion.107
  150.4 0.9 fusion.110
  151.6 0.7 copy-done.2
  152.5 17.8 %pmax.7 = f32[16,16]{0,1:T(8,128)S(1)} all-reduce(f32[16,16]{0,1:T(8,128)S(1)} %get-tuple-element.17), channel_id=1, replica_groups=mesh['groups'=2,'passage'=8,'tensor'=2] {'passage'}, use_global_device_ids=true, to_apply=%region_9.10 | all-reduce | flops 256 | bytes 2048 | tf_op jit(solution)/shard_map/pmax | solution.py:118
  170.3 1.4 fusion.32
  171.7 1.3 fusion.36
  173.1 1.4 fusion.31
  174.5 1.4 fusion.28
  176.3 0.9 fusion.22
  177.6 0.7 reshape.298
  178.4 19.1 %all-reduce.1 = f32[16,16]{0,1:T(8,128)S(1)} all-reduce(f32[16,16]{0,1:T(8,128)S(1)} %get-tuple-element.34), channel_id=3, replica_groups=mesh['groups'=2,'passage'=8,'tensor'=2] {'passage'}, use_global_device_ids=true, to_apply=%region_16.17.clone | all-reduce | flops 256 | bytes 2048
  197.8 47.7 %all-reduce.4.cloned.1.call-done = f32[16,1024]{1,0:T(8,128)} async-done(((f32[16,1024]{1,0:T(8,128)}), f32[16,1024]{1,0:T(8,128)}) %all-reduce.4.cloned.1.call-update) | async-done | bytes 65552
  245.4 1.4 fusion.87
  (72 shorter events, 7.0 us)
Async XLA Ops:
  6.5 14.7 %copy-start = (bf16[6,256,1024]{2,1,0:T(8,128)(2,1)S(1)}, bf16[6,256,1024]{2,1,0:T(8,128)(2,1)}, u32[]{:S(2)}) copy-start(bf16[6,256,1024]{2,1,0:T(8,128)(2,1)} %param.7) | copy-start | bytes 9437188
  6.5 136.3 %all-gather.3.cloned.1.call-start = ((), (), s32[]{:S(2)}) async-start(), calls=%async_computation | async-start | bytes 2359296 | tf_op jit(solution)/shard_map/all_gather | solution.py:71
  7.3 238.2 %all-reduce.4.cloned.1.call-start = ((), (), s32[]{:S(2)}) async-start(), calls=%async_computation.1 | async-start | bytes 131072
  7.3 9.5 %collective-permute-start = (bf16[128,1024]{1,0:T(8,128)(2,1)}, bf16[128,1024]{1,0:T(8,128)(2,1)S(1)}, u32[]{:S(2)}, u32[]{:S(2)}) collective-permute-start(bf16[128,1024]{1,0:T(8,128)(2,1)} %param.10), channel_id=1, source_target_pairs={{0,2},{2,0},{4,6},{6,4},{8,10},{10,8},{12,14},{14,12},{1,3},{3,1},... | collective-permute-start | bytes 786440 | tf_op jit(solution)/shard_map/ppermute | solution.py:19
  18.8 21.9 %collective-permute-start.1 = (bf16[256,1024]{1,0:T(8,128)(2,1)}, bf16[256,1024]{1,0:T(8,128)(2,1)}, u32[]{:S(2)}, u32[]{:S(2)}) collective-permute-start(bf16[256,1024]{1,0:T(8,128)(2,1)} %maximum_select_fusion.3), channel_id=1, source_target_pairs={{0,4},{2,6},{4,0},{6,2},{8,12},{10,14},{12,8},{14,10},{1,5},{3,7},... | collective-permute-start | bytes 1572872 | tf_op jit(solution)/shard_map/ppermute | solution.py:19
  21.2 149.1 %copy-start.10 = (pred[256]{0:T(512)(128)(4,1)}, pred[256]{0:T(512)(128)(4,1)S(1)}, u32[]{:S(2)}) copy-start(pred[256]{0:T(512)(128)(4,1)S(1)} %iota_compare_fusion.4) | copy-start | bytes 772
  23.6 23.3 %copy-start.14 = (bf16[2,1024]{1,0:T(2,128)(2,1)S(1)}, bf16[2,1024]{1,0:T(2,128)(2,1)}, u32[]{:S(2)}) copy-start(bf16[2,1024]{1,0:T(2,128)(2,1)} %param.8) | copy-start | bytes 12292
  23.6 105.9 %copy-start.16 = (u32[32]{0:T(128)S(1)}, u32[32]{0:T(128)}, u32[]{:S(2)}) copy-start(u32[32]{0:T(128)} %constant.73) | copy-start | bytes 388
  43.7 91.3 %collective-permute-start.2 = (bf16[512,1024]{1,0:T(8,128)(2,1)}, bf16[512,1024]{1,0:T(8,128)(2,1)}, u32[]{:S(2)}, u32[]{:S(2)}) collective-permute-start(bf16[512,1024]{1,0:T(8,128)(2,1)} %maximum_select_fusion.2), channel_id=1, source_target_pairs={{0,8},{2,10},{4,12},{6,14},{8,0},{10,2},{12,4},{14,6},{1,9},{3,11}... | collective-permute-start | bytes 3145736 | tf_op jit(solution)/shard_map/ppermute | solution.py:19
  46.9 102.3 %copy-start.15 = (pred[256]{0:T(512)(128)(4,1)}, pred[256]{0:T(512)(128)(4,1)S(1)}, u32[]{:S(2)}) copy-start(pred[256]{0:T(512)(128)(4,1)S(1)} %iota_compare_fusion.5) | copy-start | bytes 772
  131.4 18.7 %copy-start.11 = (pred[256]{0:T(512)(128)(4,1)}, pred[256]{0:T(512)(128)(4,1)S(1)}, u32[]{:S(2)}) copy-start(pred[256]{0:T(512)(128)(4,1)S(1)} %iota_compare_fusion.2) | copy-start | bytes 772
  132.1 18.3 %copy-start.12 = (pred[256]{0:T(512)(128)(4,1)}, pred[256]{0:T(512)(128)(4,1)S(1)}, u32[]{:S(2)}) copy-start(pred[256]{0:T(512)(128)(4,1)S(1)} %iota_compare_fusion.3) | copy-start | bytes 772
  132.7 18.8 %copy-start.8 = (pred[256]{0:T(512)(128)(4,1)}, pred[256]{0:T(512)(128)(4,1)S(1)}, u32[]{:S(2)}) copy-start(pred[256]{0:T(512)(128)(4,1)S(1)} %iota_compare_fusion.1) | copy-start | bytes 772
  135.0 6.3 %copy-start.1 = (bf16[1280,1024]{1,0:T(8,128)(2,1)}, bf16[1280,1024]{1,0:T(8,128)(2,1)S(1)}, u32[]{:S(2)}) copy-start(bf16[1280,1024]{1,0:T(8,128)(2,1)S(1)} %fusion) | copy-start | bytes 7864324
  151.5 0.7 copy-start.2
  170.3 5.7 %copy-start.4 = (f32[16,16,256]{2,1,0:T(8,128)S(1)}, f32[16,16,256]{2,1,0:T(8,128)}, u32[]{:S(2)}) copy-start(f32[16,16,256]{2,1,0:T(8,128)} %get-tuple-element.57) | copy-start | bytes 786436
  170.3 5.7 %copy-start.7 = (bf16[256,1024]{0,1:T(8,128)(2,1)S(1)}, bf16[256,1024]{0,1:T(8,128)(2,1)}, u32[]{:S(2)}) copy-start(bf16[256,1024]{0,1:T(8,128)(2,1)} %get-tuple-element.24) | copy-start | bytes 1572868
  170.3 5.7 %copy-start.13 = (pred[256]{0:T(512)(128)(4,1)S(1)}, pred[256]{0:T(512)(128)(4,1)}, u32[]{:S(2)}) copy-start(pred[256]{0:T(512)(128)(4,1)} %copy-done.12) | copy-start | bytes 772
  170.3 6.0 %copy-start.6 = (bf16[256,1024]{0,1:T(8,128)(2,1)S(1)}, bf16[256,1024]{0,1:T(8,128)(2,1)}, u32[]{:S(2)}) copy-start(bf16[256,1024]{0,1:T(8,128)(2,1)} %get-tuple-element.23) | copy-start | bytes 1572868
  171.7 5.5 %copy-start.3 = (f32[16,16,256]{2,1,0:T(8,128)S(1)}, f32[16,16,256]{2,1,0:T(8,128)}, u32[]{:S(2)}) copy-start(f32[16,16,256]{2,1,0:T(8,128)} %copy-done.2) | copy-start | bytes 786436
  171.7 5.5 %copy-start.5 = (bf16[256,1024]{0,1:T(8,128)(2,1)S(1)}, bf16[256,1024]{0,1:T(8,128)(2,1)}, u32[]{:S(2)}) copy-start(bf16[256,1024]{0,1:T(8,128)(2,1)} %get-tuple-element.22) | copy-start | bytes 1572868
  171.7 5.5 %copy-start.9 = (pred[256]{0:T(512)(128)(4,1)S(1)}, pred[256]{0:T(512)(128)(4,1)}, u32[]{:S(2)}) copy-start(pred[256]{0:T(512)(128)(4,1)} %copy-done.8) | copy-start | bytes 772
Sparse Core Ops, SparseCore 0:
  9.5 86.3 all-gather.2
  178.5 66.9 all-reduce.3
